TPU v7x, 256 devices: a whole 4x4x8 slice. The times are simulated.
256 devices in a mesh: dp: 8 (over z), seq: 32 (over x, y, core).
Axes of the slice: x: 4, y: 4, z: 8, core: 2. Of those that a mesh axis runs over, the one named last changes fastest.
Arguments:
- tokens: bfloat16 [128, 4, 2560], P('dp'), may hold values from -6 to 6
- attn_gain: float32 [2560], replicated, may hold values from 0.1 to 1.9
- qkv_weight: bfloat16 [3072, 2560], P(('seq', 'dp'))
- out_weight: bfloat16 [2560, 2560], P(('seq', 'dp')), may hold values from -0.125 to 0.125
- mlp_gain: float32 [2560], replicated, may hold values from 0.1 to 1.9
- gate_up: bfloat16 [2, 7680, 2560], P(None, 'seq'), may hold values from -0.125 to 0.125
- down_weight: bfloat16 [7680, 2560], P('seq'), may hold values from -0.0625 to 0.0625
- kv_pool: bfloat16 [4096, 128, 512], P(('dp', 'seq')), may hold values from -6 to 6
- cache_len: int32 [128], P('dp'), may hold values from 1 to 16384, as said below
- page_table: int32 [128, 16], P('dp'), may hold values from 0 to 511, as said below
Outputs:
- layer_out: bfloat16 [128, 4, 2560], P('dp')
- written_pool: bfloat16 [4096, 128, 512], P(('dp', 'seq'))
Inputs may be any that keep to these rules, and one draw needn't show every extreme that they name: `cache_len`: some request of the whole batch has exactly 16384 cached tokens; lengths under 2048 occur. `page_table`: within the 16 requests of one dp index all entries differ. Slot s lies on seq index s // 16; in every dp index some seq index holds exactly 16 of its pages.
All inputs are finite; a program needn't handle non-finite values.
Results may differ from a plain program's by a relative error of at most 0.018.
Values may be sent and summed in bfloat16 or wider, within the bound.
A program may use at most 128 MiB of HBM per device.

v0:
```python
import jax
import jax.numpy as jnp
from jax import lax
from jax.sharding import PartitionSpec as P

low_fill = -1e30


def rms_norm(values, gains):
    floats = values.astype(jnp.float32)
    return floats * lax.rsqrt(jnp.mean(floats * floats, axis=-1, keepdims=True) + 1e-06) * gains


def rotate(values, positions):
    quarter = values.shape[-1] // 4
    freq_index = jnp.arange(quarter).astype(jnp.float32)
    inverse = 10000.0 ** (-freq_index / quarter)
    angles = positions[..., None] * inverse
    first = values[..., :quarter]
    second = values[..., quarter : 2 * quarter]
    others = values[..., 2 * quarter :]
    cosine = jnp.cos(angles)
    sine = jnp.sin(angles)
    return jnp.concatenate(
        [first * cosine - second * sine, second * cosine + first * sine, others], axis=-1
    )


def body(
    tokens,
    attn_gain,
    qkv_weight,
    out_weight,
    mlp_gain,
    gate_up,
    down_weight,
    kv_pool,
    cache_len,
    page_table,
):
    seq_index = lax.axis_index("seq")
    requests, new_count, model_width = tokens.shape
    slot_count, page_len, pair_width = kv_pool.shape
    head_dim = pair_width // 2
    head_count = out_weight.shape[1] // head_dim
    page_count = page_table.shape[1]
    window = page_count * page_len
    row_count = requests * new_count
    query_rows = new_count * head_count
    split_q = head_count * head_dim
    scale = head_dim ** (-0.5)
    contract = (((1,), (1,)), ((), ()))
    qkv_local, out_local = (
        lax.all_gather(qkv_weight, "dp", axis=0, tiled=True),
        lax.all_gather(out_weight, "dp", axis=0, tiled=True),
    )
    normed = rms_norm(tokens, attn_gain).astype(jnp.bfloat16).reshape(row_count, model_width)
    local_part = lax.dot_general(
        normed, qkv_local, contract, preferred_element_type=jnp.float32
    ).astype(jnp.bfloat16)
    projected = lax.all_gather(local_part, "seq", axis=1, tiled=True).reshape(
        requests, new_count, -1
    )
    positions_int = cache_len[:, None] + jnp.arange(new_count, dtype=jnp.int32)[None, :]
    positions = positions_int.astype(jnp.float32)
    queries = rotate(
        projected[:, :, :split_q]
        .astype(jnp.float32)
        .reshape(requests, new_count, head_count, head_dim),
        positions[:, :, None],
    ).astype(jnp.bfloat16)
    keys_new = rotate(
        projected[:, :, split_q : split_q + head_dim].astype(jnp.float32), positions
    ).astype(jnp.bfloat16)
    values_new = projected[:, :, split_q + head_dim :]
    slot_ids = seq_index * slot_count + jnp.arange(slot_count, dtype=jnp.int32)
    matches = page_table[None, :, :] == slot_ids[:, None, None]
    owners = jnp.any(matches, axis=2)
    in_use = jnp.any(owners, axis=1)
    page_of = jnp.sum(
        jnp.where(matches, jnp.arange(page_count, dtype=jnp.int32)[None, None, :], 0), axis=(1, 2)
    )
    slot_length = jnp.sum(jnp.where(owners, cache_len[None, :], 0), axis=1)
    query_flat = queries.reshape(requests, query_rows * head_dim)
    slot_queries = jnp.dot(
        owners.astype(jnp.bfloat16), query_flat, preferred_element_type=jnp.float32
    )
    slot_queries = slot_queries.astype(jnp.bfloat16).reshape(slot_count, query_rows, head_dim)
    scores = (
        jnp.einsum(
            "pqd,pkd->pqk",
            slot_queries,
            kv_pool[:, :, :head_dim],
            preferred_element_type=jnp.float32,
        )
        * scale
    )
    cycle = page_of[:, None] * page_len + jnp.arange(page_len, dtype=jnp.int32)[None, :]
    key_pos = slot_length[:, None] - 1 - jnp.mod(slot_length[:, None] - 1 - cycle, window)
    query_pos = (
        slot_length[:, None] + (jnp.arange(query_rows, dtype=jnp.int32) // head_count)[None, :]
    )
    visible = (
        in_use[:, None, None]
        & (key_pos >= 0)[:, None, :]
        & (key_pos[:, None, :] > query_pos[:, :, None] - window)
    )
    slot_peak = jnp.max(jnp.where(visible, scores, low_fill), axis=2)
    weights = jnp.where(visible, jnp.exp(scores - slot_peak[:, :, None]), 0.0)
    slot_sum = jnp.sum(weights, axis=2)
    slot_out = jnp.einsum(
        "pqk,pkd->pqd",
        weights.astype(jnp.bfloat16),
        kv_pool[:, :, head_dim:],
        preferred_element_type=jnp.float32,
    )
    request_peak = jnp.max(jnp.where(owners[:, :, None], slot_peak[:, None, :], low_fill), axis=0)
    owner_peak = jnp.max(jnp.where(owners[:, :, None], request_peak[None, :, :], low_fill), axis=1)
    factor = jnp.exp(slot_peak - owner_peak)
    request_sum = jnp.sum(
        jnp.where(owners[:, :, None], (slot_sum * factor)[:, None, :], 0.0), axis=0
    )
    request_out = jnp.einsum(
        "pr,pqd->rqd",
        owners.astype(jnp.float32),
        slot_out * factor[:, :, None],
        precision=lax.Precision.HIGHEST,
    )
    query_block = queries.reshape(requests, query_rows, head_dim)
    new_scores = (
        jnp.einsum("rqd,rud->rqu", query_block, keys_new, preferred_element_type=jnp.float32)
        * scale
    )
    causal = jnp.arange(new_count)[None, :] <= (jnp.arange(query_rows) // head_count)[:, None]
    new_peak = jnp.max(jnp.where(causal[None], new_scores, low_fill), axis=2)
    global_peak = lax.pmax(request_peak, "seq")
    rescale = jnp.exp(request_peak - global_peak)
    old_denominator, weighted = (
        lax.psum((request_sum * rescale).astype(jnp.bfloat16), "seq").astype(jnp.float32),
        lax.psum((request_out * rescale[:, :, None]).astype(jnp.bfloat16), "seq").astype(
            jnp.float32
        ),
    )
    top_peak = jnp.maximum(global_peak, new_peak)
    new_weights = jnp.where(causal[None], jnp.exp(new_scores - top_peak[:, :, None]), 0.0)
    carried = jnp.exp(global_peak - top_peak)
    fresh_sum = jnp.sum(new_weights, axis=2)
    fresh_out = jnp.einsum(
        "rqu,rud->rqd",
        new_weights.astype(jnp.bfloat16),
        values_new,
        preferred_element_type=jnp.float32,
    )
    carried, fresh_sum, fresh_out = (carried, fresh_sum, fresh_out)
    denominator = old_denominator * carried + fresh_sum
    numerator = weighted * carried[:, :, None] + fresh_out
    attended = (
        (numerator / denominator[:, :, None]).astype(jnp.bfloat16).reshape(row_count, split_q)
    )
    heads_part = lax.dot_general(
        attended, out_local, contract, preferred_element_type=jnp.float32
    ).astype(jnp.bfloat16)
    heads_out = lax.all_gather(heads_part, "seq", axis=1, tiled=True)
    residual = (
        tokens.reshape(row_count, model_width).astype(jnp.float32) + heads_out.astype(jnp.float32)
    ).astype(jnp.bfloat16)
    hidden_in = rms_norm(residual, mlp_gain).astype(jnp.bfloat16)
    gate_and_up = jnp.einsum("rd,gfd->grf", hidden_in, gate_up, preferred_element_type=jnp.float32)
    hidden = (jax.nn.gelu(gate_and_up[0], approximate=True) * gate_and_up[1]).astype(jnp.bfloat16)
    partial_sum = jnp.dot(hidden, down_weight, preferred_element_type=jnp.float32)
    full_sum = lax.psum(partial_sum.astype(jnp.bfloat16), "seq").astype(jnp.float32)
    layer_out = (residual.astype(jnp.float32) + full_sum).astype(jnp.bfloat16)
    layer_out = layer_out.reshape(requests, new_count, model_width)
    page_index = jnp.mod(positions_int // page_len, page_count)
    slot_taken = jnp.take_along_axis(page_table, page_index, axis=1)
    local_slot = slot_taken - seq_index * slot_count
    local_slot = jnp.where((local_slot >= 0) & (local_slot < slot_count), local_slot, slot_count)
    offset = jnp.mod(positions_int, page_len)
    new_rows = jnp.concatenate([keys_new, values_new], axis=-1)
    written_pool = kv_pool.at[local_slot, offset].set(new_rows, mode="drop")
    return (layer_out, written_pool)


def solution(mesh):
    in_specs = (
        P("dp", None, None),
        P(),
        P(("seq", "dp"), None),
        P(("seq", "dp"), None),
        P(),
        P(None, "seq", None),
        P("seq", None),
        P(("dp", "seq"), None, None),
        P("dp"),
        P("dp", None),
    )
    out_specs = (P("dp", None, None), P(("dp", "seq"), None, None))
    return jax.shard_map(body, mesh=mesh, in_specs=in_specs, out_specs=out_specs, check_vma=False)
```

profile of v0, /device:TPU:1, one launch (start us, length us, event | category | flops | bytes accessed | tf_op | source)
XLA Modules:
  0.0 415.1 jit_solution(9135690108365068851)
XLA Ops:
  7.2 3.2 copy.131
  11.1 24.0 %all-gather = bf16[8,12,2560]{2,1,0:T(8,128)(2,1)S(1)} all-gather(bf16[1,12,2560]{2,1,0:T(8,128)(2,1)S(1)} %bitcast.64), channel_id=1, replica_groups=mesh['dp'=8,'seq'=32] {'dp'}, dimensions={0}, use_global_device_ids=true | all-gather | bytes 552960 | tf_op jit(solution)/shard_map/all_gather | solution.py:54
  35.1 0.9 reshape.604
  36.6 1.3 fusion.1
  37.9 31.8 %all-gather.1 = bf16[32,96,64]{1,2,0:T(8,128)(2,1)S(1)} all-gather(bf16[1,96,64]{1,2,0:T(8,128)(2,1)S(1)} %fusion.1), channel_id=1, replica_groups=mesh['dp'=8,'seq'=32] {'seq'}, dimensions={0}, use_global_device_ids=true | all-gather | bytes 405504 | tf_op jit(solution)/shard_map/all_gather | solution.py:61
  71.1 1.0 compare_reduce_fusion
  72.1 1.0 fusion.30
  74.8 0.9 copy_convert_fusion
  75.7 1.2 reshape.589
  77.0 1.0 subtract_convert_fusion.1
  79.2 0.9 convert_element_type.110
  80.2 1.2 convolution_convert_fusion
  81.8 2.4 select_reduce_fusion
  84.5 63.2 %pmax.7 = f32[16,40]{1,0:T(8,128)S(1)} all-reduce(f32[16,40]{1,0:T(8,128)S(1)} %select_reduce_fusion.3), channel_id=1, replica_groups=mesh['dp'=8,'seq'=32] {'seq'}, use_global_device_ids=true, to_apply=%region_8.9 | all-reduce | flops 640 | bytes 5120 | tf_op jit(solution)/shard_map/pmax | solution.py:136
  147.9 1.5 fusion.22
  151.4 2.1 fusion
  153.6 0.9 reshape.587
  155.2 65.4 %psum.22 = bf16[16,40]{1,0:T(8,128)(2,1)S(1)} all-reduce(bf16[16,40]{1,0:T(8,128)(2,1)S(1)} %get-tuple-element.8), channel_id=1, replica_groups=mesh['dp'=8,'seq'=32] {'seq'}, use_global_device_ids=true, to_apply=%region_13.14 | all-reduce | flops 640 | bytes 2560 | tf_op jit(solution)/shard_map/psum | solution.py:139
  222.6 20.4 %all-gather.2 = bf16[8,10,2560]{2,1,0:T(8,128)(2,1)S(1)} all-gather(bf16[1,10,2560]{2,1,0:T(8,128)(2,1)} %bitcast.65), channel_id=1, replica_groups=mesh['dp'=8,'seq'=32] {'dp'}, dimensions={0}, use_global_device_ids=true | all-gather | bytes 460800 | tf_op jit(solution)/shard_map/all_gather | solution.py:55
  243.1 0.9 reshape.608
  245.8 0.9 fusion.41
  246.7 16.8 %all-reduce.3.cloned.1.call-done = bf16[16,40,256]{2,0,1:T(8,128)(2,1)} async-done(((bf16[16,40,256]{2,0,1:T(8,128)(2,1)}), bf16[16,40,256]{2,0,1:T(8,128)(2,1)}) %all-reduce.3.cloned.1.call-update) | async-done | bytes 327696 | tf_op jit(solution)/shard_map/psum | solution.py:140
  263.5 1.3 fusion.11
  265.3 1.3 fusion.2
  266.5 23.5 %all-gather.3 = bf16[32,80,64]{1,2,0:T(8,128)(2,1)S(1)} all-gather(bf16[1,80,64]{1,2,0:T(8,128)(2,1)S(1)} %fusion.2), channel_id=1, replica_groups=mesh['dp'=8,'seq'=32] {'seq'}, dimensions={0}, use_global_device_ids=true | all-gather | bytes 337920 | tf_op jit(solution)/shard_map/all_gather | solution.py:163
  290.4 1.4 reshape.611
  291.9 1.6 fusion.5
  293.5 0.9 convolution_bitcast_fusion
  294.4 1.1 convolution_convert_fusion.1
  295.7 8.3 %scatter_fusion = bf16[16,128,512]{2,1,0:T(8,128)(2,1)} fusion(bf16[16,128,512]{2,1,0:T(8,128)(2,1)} %copy.131, s32[64]{0:T(128)S(1)} %reshape.596, bf16[64,512]{1,0:T(8,128)(2,1)S(1)} %copy-done.15), kind=kCustom, calls=%fused_computation.1 | custom fusion | bytes 197120 | tf_op jit(solution)/shard_map/scatter | solution.py:180
  304.0 102.5 %all-reduce.5.cloned.1.call-done = bf16[64,2560]{1,0:T(8,128)(2,1)} async-done(((bf16[64,2560]{1,0:T(8,128)(2,1)}), bf16[64,2560]{1,0:T(8,128)(2,1)}) %all-reduce.5.cloned.1.call-update) | async-done | bytes 327696 | tf_op jit(solution)/shard_map/psum | solution.py:171
  406.4 1.0 fusion.8
  (124 shorter events, 14.5 us)
Async XLA Ops:
  7.2 286.3 %copy-start = (bf16[2,240,2560]{2,1,0:T(8,128)(2,1)S(1)}, bf16[2,240,2560]{2,1,0:T(8,128)(2,1)}, u32[]{:S(2)}) copy-start(bf16[2,240,2560]{2,1,0:T(8,128)(2,1)} %param.15) | copy-start | bytes 7372804
  7.2 28.8 %copy-start.3 = (bf16[16,4,2560]{2,1,0:T(4,128)(2,1)S(1)}, bf16[16,4,2560]{2,1,0:T(4,128)(2,1)}, u32[]{:S(2)}) copy-start(bf16[16,4,2560]{2,1,0:T(4,128)(2,1)} %param.10) | copy-start | bytes 983044
  7.2 3.9 copy-start.16
  7.2 256.3 %all-reduce.3.cloned.1.call-start = ((), (), s32[]{:S(2)}) async-start(), calls=%async_computation | async-start | bytes 655360 | tf_op jit(solution)/shard_map/psum | solution.py:140
  10.5 25.8 %copy-start.22 = (f32[2560]{0:T(1024)S(1)}, f32[2560]{0:T(1024)}, u32[]{:S(2)}) copy-start(f32[2560]{0:T(1024)} %param.11) | copy-start | bytes 30724
  37.9 33.2 %copy-start.1 = (s32[16,16]{1,0:T(8,128)S(1)}, s32[16,16]{1,0:T(8,128)}, u32[]{:S(2)}) copy-start(s32[16,16]{1,0:T(8,128)} %param.19) | copy-start | bytes 3076
  37.9 36.3 %copy-start.23 = (s32[16]{0:T(128)S(1)}, s32[16]{0:T(128)}, u32[]{:S(2)}) copy-start(s32[16]{0:T(128)} %param.18) | copy-start | bytes 196
  70.9 3.9 copy-start.11
  77.0 1.3 copy-start.5
  78.3 0.8 copy-start.9
  78.4 3.2 copy-start.27
  78.4 3.3 copy-start.26
  78.4 3.4 copy-start.28
  79.2 68.5 %copy-start.10 = (bf16[16,4,10,64]{3,2,0,1:T(8,128)(2,1)S(1)}, bf16[16,4,10,64]{3,2,0,1:T(8,128)(2,1)}, u32[]{:S(2)}) copy-start(bf16[16,4,10,64]{3,2,0,1:T(8,128)(2,1)} %copy-done.9) | copy-start | bytes 245764
  80.1 67.6 %copy-start.8 = (bf16[16,4,10,64]{3,2,0,1:T(8,128)(2,1)S(1)}, bf16[16,4,10,64]{3,2,0,1:T(8,128)(2,1)}, u32[]{:S(2)}) copy-start(bf16[16,4,10,64]{3,2,0,1:T(8,128)(2,1)} %copy-done.7) | copy-start | bytes 245764
  80.2 67.6 %copy-start.6 = (bf16[16,4,10,128]{3,2,0,1:T(8,128)(2,1)S(1)}, bf16[16,4,10,128]{3,2,0,1:T(8,128)(2,1)}, u32[]{:S(2)}) copy-start(bf16[16,4,10,128]{3,2,0,1:T(8,128)(2,1)} %copy-done.5) | copy-start | bytes 491524
  147.7 2.0 copy-start.2
  147.7 2.0 copy-start.13
  147.8 2.6 slice-start
  147.9 2.8 copy-start.25
  149.6 1.1 copy-start.17
  149.6 1.1 copy-start.19
  149.7 3.8 copy-start.4
  151.4 92.6 %slice-start.1 = ((bf16[16,4,3072]{2,1,0:T(4,128)(2,1)}), bf16[16,4,384]{2,1,0:T(4,128)(2,1)S(1)}, s32[]{:S(2)}) async-start(bf16[16,4,3072]{2,1,0:T(4,128)(2,1)} %copy-done.11), calls=%async_computation.3 | async-start | bytes 98304 | tf_op jit(solution)/shard_map/slice | solution.py:21
  153.5 90.5 %copy-start.18 = (bf16[16,4,64]{2,1,0:T(4,128)(2,1)S(1)}, bf16[16,4,64]{2,1,0:T(4,128)(2,1)}, u32[]{:S(2)}) copy-start(bf16[16,4,64]{2,1,0:T(4,128)(2,1)} %copy-done.17) | copy-start | bytes 24580
  153.5 90.5 %copy-start.20 = (bf16[16,4,64]{2,1,0:T(4,128)(2,1)S(1)}, bf16[16,4,64]{2,1,0:T(4,128)(2,1)}, u32[]{:S(2)}) copy-start(bf16[16,4,64]{2,1,0:T(4,128)(2,1)} %copy-done.19) | copy-start | bytes 24580
  153.5 252.9 %all-reduce.5.cloned.1.call-start = ((), (), s32[]{:S(2)}) async-start(), calls=%async_computation.1 | async-start | bytes 655360 | tf_op jit(solution)/shard_map/psum | solution.py:171
  244.8 1.0 copy-start.12
  290.1 3.4 copy-start.21
  291.9 2.5 copy-start.14
  293.5 2.0 copy-start.24
  293.5 2.2 copy-start.15
  (1 other events, 0.7 us)
Sparse Core Ops, SparseCore 0:
  153.6 109.8 all-reduce.2
  295.6 110.8 all-reduce.4
where the time goes:
time: 416 us; the launch traced here: 415 us
  blocking collectives  228 us (55%)
  waiting for transfers between devices  119 us (29%)
  local copies, waits for them, and re-layouts  25.8 us (6%)
  other arithmetic  14.8 us (4%)
  between operations  14.7 us (4%)
  matrix products  12 us (3%)
    psum x1, waiting for transfers between devices, body(): lax.psum(partial_sum.astype(jnp.bfloat16), 'seq').astype(jnp.float32)  102 us
    psum x1, blocking collectives, body(): lax.psum((request_sum * rescale).astype(jnp.bfloat16), 'seq')  65.4 us
    pmax x1, blocking collectives, body(): global_peak = lax.pmax(request_peak, 'seq')  63.2 us
    all_gather x1, blocking collectives, body(): lax.all_gather(local_part, 'seq', axis=1, tiled=True)  31.8 us
    all_gather x1, blocking collectives, body(): lax.all_gather(qkv_weight, 'dp', axis=0, tiled=True)  24 us
    all_gather x1, blocking collectives, body(): heads_out = lax.all_gather(heads_part, 'seq', axis=1, tiled=True)  23.5 us
    all_gather x1, blocking collectives, body(): lax.all_gather(out_weight, 'dp', axis=0, tiled=True)  20.4 us
    psum x1, waiting for transfers between devices, body(): lax.psum((request_out * rescale[:, :, None]).astype(jnp.bfloat16), 'seq')  16.8 us
  transfers between devices with their start and end apart: 2, of which 2 were waited for; matrix products, arithmetic and copies ran while one was open for 4% of the time, Pallas kernels for 0%

commit v1 on v0

v1 whole, which is shorter than its diff:
```python
import functools

import jax
import jax.numpy as jnp
import numpy as np
from jax import lax
from jax.experimental import pallas as pl
from jax.experimental.pallas import tpu as pltpu
from jax.sharding import PartitionSpec as P

MESH = pl.DeviceIdType.MESH
LOW = -1e30
F32 = jnp.float32
BF16 = jnp.bfloat16

D = 2560
H = 10
HD = 256
PAGE = 128
WIN = 2048
NEW = 4
R = 16
NP = 16
SLOTS = 16
NZ = 8
NS = 32
ROWS = R * NEW
FFL = 240
CB = 640
RHS_T = (((1,), (1,)), ((), ()))


def iota(shape, dim):
    return lax.broadcasted_iota(jnp.int32, shape, dim)


def layer_kernel(
    tok_ref, ag_ref, qkv_ref, ow_ref, mg_ref, gu_hbm, dn_hbm, kv_hbm, len_ref, pt_ref, inv_ref,
    out_ref, new_ref,
    tokf, normed, wq, wall, wo, pj, selq, selo, cosb, sinb, bias, biasn, kv, gu, dn,
    qs, kn, vn, sc, scn, mx, lx, acc, rs_s, rs_r, emat, att, ho, resid, r2_s, r2_r,
    load_sem, zs_sem, zr_sem, os_sem, or_sem, ph_send, ph_recv,
):
    z = lax.axis_index("dp")
    s = lax.axis_index("seq")

    loads = [
        pltpu.make_async_copy(kv_hbm, kv, load_sem.at[0]),
        pltpu.make_async_copy(gu_hbm, gu, load_sem.at[1]),
        pltpu.make_async_copy(dn_hbm, dn, load_sem.at[2]),
    ]
    for copy in loads:
        copy.start()

    barrier = pltpu.get_barrier_semaphore()

    def greet_seq(i, carry):
        pl.semaphore_signal(barrier, inc=1, device_id=(z, lax.rem(s + i, NS)), device_id_type=MESH)
        return carry

    def greet_dp(i, carry):
        pl.semaphore_signal(barrier, inc=1, device_id=(lax.rem(z + i, NZ), s), device_id_type=MESH)
        return carry

    lax.fori_loop(1, NZ, greet_dp, 0)
    lax.fori_loop(1, NS, greet_seq, 0)

    tokf[...] = tok_ref[...].astype(F32)
    for t in range(NEW):
        x = tokf[:, t, :]
        y = x * lax.rsqrt(jnp.mean(x * x, axis=-1, keepdims=True) + 1e-06) * ag_ref[...]
        normed[pl.ds(R * t, R), :] = y.astype(BF16)

    pl.semaphore_wait(barrier, NZ - 1 + NS - 1)

    up = lax.rem(z + 1, NZ)
    down = lax.rem(z + NZ - 1, NZ)
    half = D // 2

    def ring(direction, step, chunk):
        cols = pl.ds(chunk * half, half)
        if direction == 0:
            src = qkv_ref if step == 1 else wq.at[NZ - (step - 1)]
            dst, peer = wq.at[NZ - step], up
        else:
            src = qkv_ref if step == 1 else wq.at[step - 1]
            dst, peer = wq.at[step], down
        return pltpu.make_async_remote_copy(
            src_ref=src.at[:, cols],
            dst_ref=dst.at[:, cols],
            send_sem=zs_sem.at[direction, step - 1, chunk],
            recv_sem=zr_sem.at[direction, step - 1, chunk],
            device_id=(peer, s),
            device_id_type=MESH,
        )

    def carried(direction, step, chunk):
        return step < 4 or chunk == direction

    for chunk in range(2):
        for direction in range(2):
            ring(direction, 1, chunk).start()

    def pass_on(step):
        for chunk in range(2):
            for direction in range(2):
                if carried(direction, step, chunk):
                    ring(direction, step, chunk).wait_recv()
                    if step < 4 and carried(direction, step + 1, chunk):
                        ring(direction, step + 1, chunk).start()

    wall[...] = jnp.zeros_like(wall)
    wall[0, pl.ds(0, 12), :] = qkv_ref[...]

    lens = jnp.zeros((R, 1), jnp.int32)
    row_id = iota((R, 1), 0)
    for r in range(R):
        lens = jnp.where(row_id == r, len_ref[r], lens)
    for t in range(NEW):
        angle = (lens + t).astype(F32) * inv_ref[...]
        cosine = jnp.cos(angle)
        sine = jnp.sin(angle)
        sign = jnp.where(iota((R, 128), 1) < 64, -1.0, 1.0)
        cosb[pl.ds(R * t, R), :] = cosine
        sinb[pl.ds(R * t, R), :] = sine * sign

    pass_on(1)
    for c in range(4):
        rows = iota((128, 384), 0)
        part = rows % 16
        target = 96 * c + 12 * ((rows // 16 + z) % NZ) + part
        hit = (target == iota((128, 384), 1)) & (part < 12)
        selq[pl.ds(128 * c, 128), :] = jnp.where(hit, 1.0, 0.0).astype(BF16)
    wall[NZ - 1, pl.ds(0, 12), :] = wq[NZ - 1]
    wall[1, pl.ds(0, 12), :] = wq[1]
    pass_on(2)
    wall[NZ - 2, pl.ds(0, 12), :] = wq[NZ - 2]
    wall[2, pl.ds(0, 12), :] = wq[2]

    local = pt_ref[...] - s * SLOTS

    def mask_block(kb, carry):
        lane = iota((R, 256), 1)
        slot = kb * 2 + lane // PAGE
        page = jnp.full((R, 256), -1, jnp.int32)
        for i in range(NP):
            page = jnp.where(local[:, i : i + 1] == slot, i, page)
        last = lens - 1
        key_pos = last - ((last - (page * PAGE + lane % PAGE)) & (WIN - 1))
        fine = (page >= 0) & (key_pos >= 0)
        for t in range(NEW):
            seen = fine & (key_pos > lens + (t - WIN))
            bias[kb, pl.ds(R * t, R), :] = jnp.where(seen, 0.0, LOW)
        return carry

    lax.fori_loop(0, 8, mask_block, 0)
    key_id = iota((R, 128), 1)
    for t in range(NEW):
        seen = (key_id < ROWS) & (key_id % R == iota((R, 128), 0)) & (key_id // R <= t) & (s == 0)
        biasn[pl.ds(R * t, R), :] = jnp.where(seen, 0.0, LOW)

    pass_on(3)
    wall[NZ - 3, pl.ds(0, 12), :] = wq[NZ - 3]
    wall[3, pl.ds(0, 12), :] = wq[3]
    pass_on(4)
    wall[4, pl.ds(0, 12), :] = wq[4]

    def send_out(i):
        return pltpu.make_async_remote_copy(
            src_ref=ow_ref,
            dst_ref=wo.at[NZ - i],
            send_sem=os_sem,
            recv_sem=or_sem,
            device_id=(lax.rem(z + i, NZ), s),
            device_id_type=MESH,
        )

    def start_out(i, carry):
        send_out(i).start()
        return carry

    lax.fori_loop(1, NZ, start_out, 0)

    def gather_copy(phase, buf, i):
        return pltpu.make_async_remote_copy(
            src_ref=buf.at[s],
            dst_ref=buf.at[s],
            send_sem=ph_send.at[phase],
            recv_sem=ph_recv.at[phase],
            device_id=(z, lax.rem(s + i, NS)),
            device_id_type=MESH,
        )

    def scatter_copy(phase, src, dst, i):
        peer = lax.rem(s + i, NS)
        return pltpu.make_async_remote_copy(
            src_ref=src.at[peer],
            dst_ref=dst.at[s],
            send_sem=ph_send.at[phase],
            recv_sem=ph_recv.at[phase],
            device_id=(z, peer),
            device_id_type=MESH,
        )

    def start_all(make):
        def one(i, carry):
            make(i).start()
            return carry

        lax.fori_loop(1, NS, one, 0)

    def wait_bytes(ref, sem):
        pltpu.make_async_copy(ref, ref, sem).wait()

    def received(phase, buf):
        wait_bytes(buf.at[pl.ds(0, NS - 1)], ph_recv.at[phase])

    def sent(phase, buf):
        wait_bytes(buf.at[pl.ds(0, NS - 1)], ph_send.at[phase])

    part = lax.dot_general(
        normed[...], wall[...].reshape(128, D), RHS_T, preferred_element_type=F32
    )
    pj[s] = part.astype(BF16)
    start_all(functools.partial(gather_copy, 0, pj))
    for c in range(8):
        rows = iota((128, CB), 0)
        lanes = rows % 16
        target = 80 * c + 10 * ((rows // 16 + z) % NZ) + lanes
        hit = (target == iota((128, CB), 1)) & (lanes < 10)
        selo[pl.ds(128 * c, 128), :] = jnp.where(hit, 1.0, 0.0).astype(BF16)
    col_block = lax.rem(s, 4)
    lane = iota((128, CB), 0)
    head_of = (col_block * 5 + iota((128, CB), 1) // 128) // 2
    emat[...] = jnp.where((lane % 16 == head_of) & (lane < 48), 1.0, 0.0).astype(BF16)
    kn[...] = jnp.zeros_like(kn)
    vn[...] = jnp.zeros_like(vn)
    loads[0].wait()
    received(0, pj)

    groups = jnp.concatenate(
        [pj[...].reshape(8, 4, ROWS, 128)[:, c].reshape(8 * ROWS, 128) for c in range(4)], axis=1
    )
    proj = jnp.dot(groups, selq[...], preferred_element_type=F32)

    def unit(u):
        g, c = u // 3, u % 3
        return proj[ROWS * g : ROWS * (g + 1), 128 * c : 128 * (c + 1)]

    def turned(v):
        return v * cosb[...] + pltpu.roll(v, 64, 1) * sinb[...]

    for h in range(H):
        qs[pl.ds(ROWS * h, ROWS), pl.ds(0, 128)] = (
            turned(unit(2 * h)).astype(BF16) * jnp.asarray(HD ** -0.5, BF16)
        )
        qs[pl.ds(ROWS * h, ROWS), pl.ds(128, 128)] = (
            unit(2 * h + 1).astype(BF16) * jnp.asarray(HD ** -0.5, BF16)
        )
    kn[pl.ds(0, ROWS), pl.ds(0, 128)] = turned(unit(20)).astype(BF16)
    kn[pl.ds(0, ROWS), pl.ds(128, 128)] = unit(21).astype(BF16)
    vn[pl.ds(0, ROWS), pl.ds(0, 128)] = unit(22).astype(BF16)
    vn[pl.ds(0, ROWS), pl.ds(128, 128)] = unit(23).astype(BF16)
    new_ref[:, pl.ds(0, HD)] = kn[pl.ds(0, ROWS), :].astype(F32)
    new_ref[:, pl.ds(HD, HD)] = vn[pl.ds(0, ROWS), :].astype(F32)

    score_n = lax.dot_general(qs[...], kn[...], RHS_T, preferred_element_type=F32)
    score_n = (score_n.reshape(H, ROWS, 128) + biasn[...][None]).reshape(H * ROWS, 128)
    scn[...] = score_n
    mx[...] = score_n

    def score_block(kb, carry):
        keys = kv[pl.ds(kb * 2, 2), :, pl.ds(0, HD)].reshape(256, HD)
        value = lax.dot_general(qs[...], keys, RHS_T, preferred_element_type=F32)
        value = (value.reshape(H, ROWS, 256) + bias[kb][None]).reshape(H * ROWS, 256)
        sc[kb] = value
        mx[...] = jnp.maximum(mx[...], jnp.maximum(value[:, :128], value[:, 128:]))
        return carry

    lax.fori_loop(0, 8, score_block, 0)
    peak = jnp.max(mx[...], axis=1, keepdims=True)
    mx[...] = jnp.broadcast_to(peak, mx.shape)
    weight = jnp.exp(scn[...] - mx[...])
    lx[...] = weight
    acc[...] = jnp.dot(weight.astype(BF16), vn[...], preferred_element_type=F32)

    def value_block(kb, carry):
        left = jnp.exp(sc[kb, :, pl.ds(0, 128)] - mx[...])
        right = jnp.exp(sc[kb, :, pl.ds(128, 128)] - mx[...])
        lx[...] += left + right
        both = jnp.concatenate([left.astype(BF16), right.astype(BF16)], axis=1)
        values = kv[pl.ds(kb * 2, 2), :, pl.ds(HD, HD)].reshape(256, HD)
        acc[...] += jnp.dot(both, values, preferred_element_type=F32)
        return carry

    lax.fori_loop(0, 8, value_block, 0)
    total = jnp.sum(lx[...], axis=1, keepdims=True)
    level = mx[...] + jnp.log(jnp.broadcast_to(total, mx.shape))
    mixed = acc[...] / total
    lane_h = iota((ROWS, 128), 1)
    table = jnp.zeros((ROWS, 128), F32)
    for h in range(H):
        table = jnp.where(lane_h % 16 == h, level[ROWS * h : ROWS * (h + 1)], table)
        for side in range(2):
            u = 2 * h + side
            piece = mixed[ROWS * h : ROWS * (h + 1), 128 * side : 128 * (side + 1)]
            rs_s[:, u // 5, :, pl.ds(128 * (u % 5), 128)] = piece.reshape(8, 8, 128).astype(BF16)
    first = table.astype(BF16).astype(F32)
    second = (table - first).astype(BF16).astype(F32)
    third = table - first - second
    table = jnp.where(lane_h < 16, first, jnp.where(lane_h < 32, second, third))
    table = jnp.where(lane_h % 16 < H, table, 0.0).reshape(8, 8, 128).astype(BF16)
    for c in range(4):
        rs_s[:, c, :, pl.ds(CB, 128)] = table

    def flat(ref):
        return ref

    def part_copy(i):
        peer = lax.rem(s + i, NS)
        return pltpu.make_async_remote_copy(
            src_ref=rs_s.at[peer // 4, peer % 4],
            dst_ref=rs_r.at[s],
            send_sem=ph_send.at[1],
            recv_sem=ph_recv.at[1],
            device_id=(z, peer),
            device_id_type=MESH,
        )

    start_all(part_copy)
    rs_r[s] = rs_s[s // 4, s % 4]
    received(1, rs_r)
    levels = rs_r[:, :, pl.ds(CB, 128)].astype(F32).reshape(NS * 8, 128).astype(BF16)
    levels = jnp.dot(levels, emat[...], preferred_element_type=F32).reshape(NS, 8, CB)
    factor = jnp.exp(levels - jnp.max(levels, axis=0, keepdims=True))
    number = jnp.sum(factor * rs_r[:, :, pl.ds(0, CB)].astype(F32), axis=0)
    attended = number / jnp.sum(factor, axis=0)

    att[s] = attended.astype(BF16)
    start_all(functools.partial(gather_copy, 2, att))
    wait_bytes(wo.at[pl.ds(1, NZ - 1)], or_sem)
    wall[...] = jnp.zeros_like(wall)
    wall[0, pl.ds(0, 10), :] = ow_ref[...]
    for d in range(1, NZ):
        wall[d, pl.ds(0, 10), :] = wo[d]
    received(2, att)
    rows_att = att[...].astype(F32).reshape(8, 4, 8, CB)
    part = jnp.zeros((ROWS, 128), F32)
    for c in range(4):
        left = rows_att[:, c].reshape(ROWS, CB).astype(BF16)
        part += lax.dot_general(
            left, wall[:, :, pl.ds(CB * c, CB)].reshape(128, CB), RHS_T, preferred_element_type=F32
        )

    ho[s] = part.astype(BF16)
    start_all(functools.partial(gather_copy, 3, ho))
    loads[1].wait()
    loads[2].wait()
    received(3, ho)
    groups = jnp.concatenate(
        [ho[...].reshape(4, 8, ROWS, 128)[:, c].reshape(4 * ROWS, 128) for c in range(8)], axis=1
    )
    heads_out = jnp.dot(groups, selo[...], preferred_element_type=F32)
    square = jnp.zeros((ROWS, 1), F32)
    pieces = []
    for c in range(4):
        cols = pl.ds(CB * c, CB)
        x = jnp.concatenate([tokf[:, t, cols] for t in range(NEW)], axis=0)
        x = (x + heads_out[ROWS * c : ROWS * (c + 1)]).astype(BF16).astype(F32)
        pieces.append(x)
        resid[:, c] = x.reshape(8, 8, CB)
        square += jnp.sum(x * x, axis=1, keepdims=True)
    scale = lax.rsqrt(square * (1.0 / D) + 1e-06)
    gate = jnp.zeros((ROWS, FFL), F32)
    lift = jnp.zeros((ROWS, FFL), F32)
    for c in range(4):
        cols = pl.ds(CB * c, CB)
        entry = (pieces[c] * scale * mg_ref[:, cols]).astype(BF16)
        gate += lax.dot_general(entry, gu[0, :, cols], RHS_T, preferred_element_type=F32)
        lift += lax.dot_general(entry, gu[1, :, cols], RHS_T, preferred_element_type=F32)
    inner = np.float32(np.sqrt(2.0 / np.pi)) * (gate + 0.044715 * (gate * gate * gate))
    hidden = (0.5 * gate * (1.0 + jnp.tanh(inner)) * lift).astype(BF16)
    for c in range(4):
        value = jnp.dot(hidden, dn[:, pl.ds(CB * c, CB)], preferred_element_type=F32)
        r2_s[:, c] = value.reshape(8, 8, CB).astype(BF16)

    def sum_copy(i):
        peer = lax.rem(s + i, NS)
        return pltpu.make_async_remote_copy(
            src_ref=r2_s.at[peer // 4, peer % 4],
            dst_ref=r2_r.at[s],
            send_sem=ph_send.at[4],
            recv_sem=ph_recv.at[4],
            device_id=(z, peer),
            device_id_type=MESH,
        )

    start_all(sum_copy)
    r2_r[s] = r2_s[s // 4, s % 4]
    received(4, r2_r)
    done = jnp.sum(r2_r[...].astype(F32), axis=0) + resid[s // 4, s % 4]

    out_ref[s] = done.astype(BF16)
    start_all(functools.partial(gather_copy, 5, out_ref))
    for direction in range(2):
        for step in range(1, 5):
            for chunk in range(2):
                if carried(direction, step, chunk):
                    ring(direction, step, chunk).wait_send()
    wait_bytes(wo.at[pl.ds(1, NZ - 1)], os_sem)
    sent(0, pj)
    sent(1, rs_r)
    sent(2, att)
    sent(3, ho)
    sent(4, r2_r)
    received(5, out_ref)
    sent(5, out_ref)


def write_kernel(s_ref, len_ref, pt_ref, kv_hbm, new_ref, out_hbm, pool, in_sem, out_sem):
    s = s_ref[0]
    copies = [pltpu.make_async_copy(kv_hbm.at[p], pool.at[p], in_sem.at[p]) for p in range(SLOTS)]
    for copy in copies:
        copy.start()
    for copy in copies:
        copy.wait()

    def one(n, carry):
        r = n // NEW
        t = n % NEW
        pos = len_ref[r] + t
        slot = pt_ref[r, (pos // PAGE) % NP] - s * SLOTS

        @pl.when((slot >= 0) & (slot < SLOTS))
        def _():
            place = pos % PAGE
            base = pl.multiple_of((place // 16) * 16, 16)
            old = pool[slot, pl.ds(base, 16), :].astype(F32)
            row = new_ref[pl.ds(t * R + r, 1), :]
            mixed = jnp.where(iota((16, 2 * HD), 0) == place - base, row, old)
            pool[slot, pl.ds(base, 16), :] = mixed.astype(BF16)

        return carry

    lax.fori_loop(0, ROWS, one, 0)
    copies = [pltpu.make_async_copy(pool.at[p], out_hbm.at[p], out_sem.at[p]) for p in range(SLOTS)]
    for copy in copies:
        copy.start()
    for copy in copies:
        copy.wait()


def body(
    tokens,
    attn_gain,
    qkv_weight,
    out_weight,
    mlp_gain,
    gate_up,
    down_weight,
    kv_pool,
    cache_len,
    page_table,
):
    freq = np.arange(64, dtype=np.float64)
    inverse = (10000.0 ** (-freq / 64)).astype(np.float32)
    inverse = jnp.asarray(np.concatenate([inverse, inverse])[None, :])
    vmem = pl.BlockSpec(memory_space=pltpu.VMEM)
    smem = pl.BlockSpec(memory_space=pltpu.SMEM)
    hbm = pl.BlockSpec(memory_space=pl.ANY)
    dma = pltpu.SemaphoreType.DMA
    blocks, new_rows = pl.pallas_call(
        layer_kernel,
        out_shape=(
            jax.ShapeDtypeStruct((NS, 8, CB), BF16),
            jax.ShapeDtypeStruct((ROWS, 2 * HD), F32),
        ),
        in_specs=[vmem] * 5 + [hbm] * 3 + [smem, vmem, vmem],
        out_specs=(vmem, vmem),
        scratch_shapes=[
            pltpu.VMEM((R, NEW, D), F32),
            pltpu.VMEM((ROWS, D), BF16),
            pltpu.VMEM((NZ, 12, D), BF16),
            pltpu.VMEM((NZ, 16, D), BF16),
            pltpu.VMEM((NZ, 10, D), BF16),
            pltpu.VMEM((NS, ROWS, 128), BF16),
            pltpu.VMEM((512, 384), BF16),
            pltpu.VMEM((1024, CB), BF16),
            pltpu.VMEM((ROWS, 128), F32),
            pltpu.VMEM((ROWS, 128), F32),
            pltpu.VMEM((8, ROWS, 256), F32),
            pltpu.VMEM((ROWS, 128), F32),
            pltpu.VMEM((SLOTS, PAGE, 2 * HD), BF16),
            pltpu.VMEM((2, FFL, D), BF16),
            pltpu.VMEM((FFL, D), BF16),
            pltpu.VMEM((H * ROWS, HD), BF16),
            pltpu.VMEM((128, HD), BF16),
            pltpu.VMEM((128, HD), BF16),
            pltpu.VMEM((8, H * ROWS, 256), F32),
            pltpu.VMEM((H * ROWS, 128), F32),
            pltpu.VMEM((H * ROWS, 128), F32),
            pltpu.VMEM((H * ROWS, 128), F32),
            pltpu.VMEM((H * ROWS, HD), F32),
            pltpu.VMEM((8, 4, 8, CB + 128), BF16),
            pltpu.VMEM((NS, 8, CB + 128), BF16),
            pltpu.VMEM((128, CB), BF16),
            pltpu.VMEM((NS, 8, CB), BF16),
            pltpu.VMEM((NS, ROWS, 128), BF16),
            pltpu.VMEM((8, 4, 8, CB), F32),
            pltpu.VMEM((8, 4, 8, CB), BF16),
            pltpu.VMEM((NS, 8, CB), BF16),
            dma((3,)),
            dma((2, 4, 2)),
            dma((2, 4, 2)),
            dma(()),
            dma(()),
            dma((6,)),
            dma((6,)),
        ],
        compiler_params=pltpu.CompilerParams(
            collective_id=0, has_side_effects=True, vmem_limit_bytes=60 * 1024 * 1024
        ),
        name="layer",
    )(
        tokens,
        attn_gain.reshape(1, D),
        qkv_weight,
        out_weight,
        mlp_gain.reshape(1, D),
        gate_up,
        down_weight,
        kv_pool,
        cache_len,
        page_table,
        inverse,
    )
    written_pool = pl.pallas_call(
        write_kernel,
        out_shape=jax.ShapeDtypeStruct((SLOTS, PAGE, 2 * HD), BF16),
        in_specs=[smem, smem, smem, hbm, vmem],
        out_specs=hbm,
        scratch_shapes=[pltpu.VMEM((SLOTS, PAGE, 2 * HD), BF16), dma((SLOTS,)), dma((SLOTS,))],
        name="write",
    )(lax.axis_index("seq").reshape(1), cache_len, page_table, kv_pool, new_rows)
    layer_out = blocks.reshape(4, 2, 4, 8, CB).transpose(1, 3, 0, 2, 4).reshape(R, NEW, D)
    return (layer_out, written_pool)


def solution(mesh):
    in_specs = (
        P("dp", None, None),
        P(),
        P(("seq", "dp"), None),
        P(("seq", "dp"), None),
        P(),
        P(None, "seq", None),
        P("seq", None),
        P(("dp", "seq"), None, None),
        P("dp"),
        P("dp", None),
    )
    out_specs = (P("dp", None, None), P(("dp", "seq"), None, None))
    return jax.shard_map(body, mesh=mesh, in_specs=in_specs, out_specs=out_specs, check_vma=False)
```

time: 416 us -> 94.4 us (0.23)
  blocking collectives: 228 us -> 0 us
  waiting for transfers between devices: 119 us -> 0 us
  Pallas kernels: 0 us -> 88.8 us
  local copies, waits for them, and re-layouts: 25.8 us -> 4.57 us
  other arithmetic: 14.8 us -> 0 us
  between operations: 14.7 us -> 0.65 us
  matrix products: 12 us -> 0 us
    psum x2 -> x0, waiting for transfers between devices: 119 us -> none  [the longest x1 102 us: body(): lax.psum(partial_sum.astype(jnp.bfloat16), 'seq').astype(jnp.float32)]
    all_gather x4 -> x0, blocking collectives: 99.8 us -> none  [the longest x1 31.8 us: body(): lax.all_gather(local_part, 'seq', axis=1, tiled=True)]
    pallas_call x0 -> x2, Pallas kernels: none -> 88.8 us  [the longest x1 82.6 us: body(): pl.pallas_call(layer_kernel, out_shape=(jax.ShapeDtypeStruct((NS, 8, CB),...]
    psum x1 -> x0, blocking collectives: 65.4 us -> none  [body(): lax.psum((request_sum * rescale).astype(jnp.bfloat16), 'seq')]
    pmax x1 -> x0, blocking collectives: 63.2 us -> none  [body(): global_peak = lax.pmax(request_peak, 'seq')]
    dot_general x10 -> x0, matrix products: 12 us -> none  [the longest x1 2.43 us: body(): jnp.einsum('pqd,pkd->pqk', slot_queries, kv_pool[:, :, :head_dim], prefer...]
    scatter x1 -> x0, local copies, waits for them, and re-layouts: 8.32 us -> none  [body(): written_pool = kv_pool.at[local_slot, offset].set(new_rows, mode='drop')]
    unnamed x63 -> x0, local copies, waits for them, and re-layouts: 6.51 us -> none
  transfers between devices with their start and end apart: 2 -> 0, of which waited for: 2 -> 0; matrix products, arithmetic and copies ran while one was open for 4% -> 0% of each run, Pallas kernels for 0% -> 0%
where the time goes in v1:
time: 94.4 us; the launch traced here: 94 us
  Pallas kernels  88.8 us (94%)
  local copies, waits for them, and re-layouts  4.57 us (5%)
    pallas_call x1, Pallas kernels, body(): pl.pallas_call(layer_kernel, out_shape=(jax.ShapeDtypeStruct((NS, 8, CB),...  82.6 us
    pallas_call x1, Pallas kernels, body(): pl.pallas_call(write_kernel, out_shape=jax.ShapeDtypeStruct((SLOTS, PAGE,...  6.14 us

profile of v1, /device:TPU:1, one launch (start us, length us, event | category | flops | bytes accessed | tf_op | source)
XLA Modules:
  0.0 94.0 jit_solution(7028911492195569018)
XLA Ops:
  0.6 1.3 %reshape.19.ag_ref = f32[1,2560]{1,0:T(1,128)} reshape(f32[2560]{0:T(1024)} %param.12) | data formatting | bytes 20480 | tf_op jit(solution)/shard_map/reshape | solution.py:526
  1.9 1.3 %reshape.20.mg_ref = f32[1,2560]{1,0:T(1,128)} reshape(f32[2560]{0:T(1024)} %param.15) | data formatting | bytes 20480 | tf_op jit(solution)/shard_map/reshape | solution.py:529
  3.3 82.6 %layer.1 = (bf16[32,8,640]{2,1,0:T(8,128)(2,1)}, f32[64,512]{1,0:T(8,128)}) custom-call(bf16[16,4,2560]{2,1,0:T(4,128)(2,1)} %tok_ref.1, f32[1,2560]{1,0:T(1,128)} %reshape.19.ag_ref, bf16[12,2560]{1,0:T(8,128)(2,1)} %qkv_ref.1, bf16[10,2560]{1,0:T(8,128)(2,1)} %ow_ref.1, f32[1,2560]{1,0:T(1,128)} %reshape.20.mg_ref, bf16[2,240,2560]{2,1,0:T(8,128)(2,1)} %gu_hbm.1, ...), custom_call_target="tpu_custom_call" | custom-call | tf_op jit(solution)/shard_map/layer/pallas_call | solution.py:472
  85.9 1.1 %copy.13 = bf16[2,8,4,4,640]{4,3,2,1,0:T(4,128)(2,1)S(1)} copy(bf16[2,8,4,4,640]{4,1,3,0,2:T(8,128)(2,1)} %bitcast.4) | data formatting | bytes 655360 | tf_op jit(solution)/shard_map/transpose | solution.py:545
  87.0 0.8 reshape.22
  87.9 6.1 %write.1 = bf16[16,128,512]{2,1,0:T(8,128)(2,1)} custom-call(s32[1]{0:T(128)} %bitcast.2.s_ref, s32[16]{0:T(128)} %len_ref.3, s32[16,16]{1,0:T(8,128)} %pt_ref.3, bf16[16,128,512]{2,1,0:T(8,128)(2,1)} %kv_hbm.3, f32[64,512]{1,0:T(8,128)} %get-tuple-element.5.new_ref), custom_call_target="tpu_custom_call" | custom-call | tf_op jit(solution)/shard_map/write/pallas_call | solution.py:537

commit v2 on v1

v2 whole, which is shorter than its diff:
```python
import functools

import jax
import jax.numpy as jnp
import numpy as np
from jax import lax
from jax.experimental import pallas as pl
from jax.experimental.pallas import tpu as pltpu
from jax.sharding import PartitionSpec as P

MESH = pl.DeviceIdType.MESH
LOW = -1e30
F32 = jnp.float32
BF16 = jnp.bfloat16

D = 2560
H = 10
HD = 256
PAGE = 128
WIN = 2048
NEW = 4
R = 16
NP = 16
SLOTS = 16
NZ = 8
NS = 32
ROWS = R * NEW
FFL = 240
CB = 640
RHS_T = (((1,), (1,)), ((), ()))


def iota(shape, dim):
    return lax.broadcasted_iota(jnp.int32, shape, dim)


OFFSETS = sorted(
    [(dx, dy) for dx in range(4) for dy in range(4) if dx + dy > 0],
    key=lambda o: min(o[0], 4 - o[0]) + min(o[1], 4 - o[1]),
)


def layer_kernel(
    tok_ref, ag_ref, qkv_ref, ow_ref, mg_ref, gu_hbm, dn_hbm, kv_hbm, len_ref, pt_ref, inv_ref,
    out_ref, pool_ref,
    tokf, tokr, normed, wq, wall, wo, pj, selq, selo, cosb, sinb, bias, biasn, place, kv, gu, dn,
    qs, kn, vn, fresh, sc, scn, mx, lx, acc, rs_s, rs_r, emat, att, ho, resid, r2_s, r2_r,
    load_sem, zs_sem, zr_sem, os_sem, or_sem, ph_send, ph_recv, near_recv, pair_recv,
):
    z = lax.axis_index("dp")
    s = lax.axis_index("seq")
    chip, core = s // 2, lax.rem(s, 2)
    chip_x, chip_y = chip // 4, lax.rem(chip, 4)

    loads = [
        pltpu.make_async_copy(kv_hbm, kv, load_sem.at[0]),
        pltpu.make_async_copy(gu_hbm, gu, load_sem.at[1]),
        pltpu.make_async_copy(dn_hbm, dn, load_sem.at[2]),
    ]
    barrier = pltpu.get_barrier_semaphore()

    def greet_seq(i, carry):
        pl.semaphore_signal(barrier, inc=1, device_id=(z, lax.rem(s + i, NS)), device_id_type=MESH)
        return carry

    def greet_dp(i, carry):
        pl.semaphore_signal(barrier, inc=1, device_id=(lax.rem(z + i, NZ), s), device_id_type=MESH)
        return carry

    lax.fori_loop(1, NZ, greet_dp, 0)
    lax.fori_loop(1, NS, greet_seq, 0)
    for copy in loads:
        copy.start()

    def gains(ref):
        return jnp.concatenate([ref[i : i + 1, :] for i in range(D // 128)], axis=1)

    tokf[...] = tok_ref[...].astype(F32)
    by_token = jnp.concatenate([tokf[:, t, :] for t in range(NEW)], axis=0).astype(BF16)
    rows, cols = iota((ROWS, ROWS), 0), iota((ROWS, ROWS), 1)
    order = (cols // R == rows % NEW) & (cols % R == rows // NEW)
    tokr[...] = jnp.dot(
        jnp.where(order, 1.0, 0.0).astype(BF16), by_token, preferred_element_type=F32
    )
    gain = gains(ag_ref)
    for b in range(4):
        x = tokr[pl.ds(16 * b, 16), :]
        y = x * lax.rsqrt(jnp.mean(x * x, axis=-1, keepdims=True) + 1e-06) * gain
        normed[pl.ds(16 * b, 16), :] = y.astype(BF16)

    row_id = iota((ROWS, 1), 0)
    lens = jnp.zeros((ROWS, 1), jnp.int32)
    table_pages = jnp.zeros((ROWS, NP), jnp.int32)
    for r in range(R):
        mine = row_id // NEW == r
        lens = jnp.where(mine, len_ref[r], lens)
        table_pages = jnp.where(mine, pt_ref[r : r + 1, :], table_pages)
    token = row_id % NEW
    pos = lens + token

    pl.semaphore_wait(barrier, NZ - 1 + NS - 1)

    half = D // 2

    def hop(src, buf, sems, sign, away, chunk):
        send, recv = sems
        own = away <= 2
        came = NZ - 2 if sign > 0 else 2
        dist = away if own else away - 2
        slot = NZ - away if sign > 0 else away
        cols = pl.ds(chunk * half, half)
        side = 0 if sign > 0 else 1
        ref = src if own else buf.at[came]
        return pltpu.make_async_remote_copy(
            src_ref=ref.at[:, cols],
            dst_ref=buf.at[slot].at[:, cols],
            send_sem=send.at[side, away - 1, chunk],
            recv_sem=recv.at[side, away - 1, chunk],
            device_id=(lax.rem(z + NZ + sign * dist, NZ), s),
            device_id_type=MESH,
        )

    def chunks(sign, away):
        return (0, 1) if away < 4 else ((0,) if sign > 0 else (1,))

    q_hop = functools.partial(hop, qkv_ref, wq, (zs_sem, zr_sem))
    o_hop = functools.partial(hop, ow_ref, wo, (os_sem, or_sem))

    def send_own(move):
        for away in (2, 1):
            for i in range(2):
                for sign in (1, -1):
                    chunk = i if sign > 0 else 1 - i
                    move(sign, away, chunk).start()

    def send_on(move):
        for i in range(2):
            for sign in (1, -1):
                chunk = i if sign > 0 else 1 - i
                move(sign, 2, chunk).wait_recv()
                for away in (4, 3):
                    if chunk in chunks(sign, away):
                        move(sign, away, chunk).start()

    def arrived(move, away):
        for sign in (1, -1):
            for chunk in chunks(sign, away):
                move(sign, away, chunk).wait_recv()

    def left(move):
        for away in range(1, 5):
            for sign in (1, -1):
                for chunk in chunks(sign, away):
                    move(sign, away, chunk).wait_send()

    send_own(q_hop)

    angle = pos.astype(F32) * inv_ref[...]
    cosb[...] = jnp.cos(angle)
    sinb[...] = jnp.sin(angle) * jnp.where(iota((ROWS, 128), 1) < 64, -1.0, 1.0)
    wall[...] = jnp.zeros_like(wall)
    wall[0, pl.ds(0, 12), :] = qkv_ref[...]

    send_on(q_hop)

    for c in range(4):
        rows = iota((128, 384), 0)
        part = rows % 16
        target = 96 * c + 12 * ((rows // 16 + z) % NZ) + part
        hit = (target == iota((128, 384), 1)) & (part < 12)
        selq[pl.ds(128 * c, 128), :] = jnp.where(hit, 1.0, 0.0).astype(BF16)
    arrived(q_hop, 1)
    for d in (1, 2, 6, 7):
        wall[d, pl.ds(0, 12), :] = wq[d]

    local = table_pages - s * SLOTS

    def mask_block(kb, carry):
        lane = iota((ROWS, 256), 1)
        slot = kb * 2 + lane // PAGE
        page = jnp.full((ROWS, 256), -1, jnp.int32)
        for i in range(NP):
            page = jnp.where(local[:, i : i + 1] == slot, i, page)
        last = lens - 1
        cycle = page * PAGE + lane % PAGE
        key_pos = last - ((last - cycle) & (WIN - 1))
        seen = (page >= 0) & (key_pos >= 0) & (key_pos > pos - WIN)
        bias[kb] = jnp.where(seen, 0.0, LOW)
        place[kb] = jnp.where(cycle == (pos & (WIN - 1)), 1.0, 0.0).astype(BF16)
        return carry

    lax.fori_loop(0, 8, mask_block, 0)
    key_id = iota((ROWS, 128), 1)
    seen = (key_id // NEW == row_id // NEW) & (key_id % NEW <= token) & (s == 0)
    biasn[...] = jnp.where(seen, 0.0, LOW)

    arrived(q_hop, 3)
    arrived(q_hop, 4)
    for d in (3, 4, 5):
        wall[d, pl.ds(0, 12), :] = wq[d]

    def wait_bytes(ref, sem):
        pltpu.make_async_copy(ref, ref, sem).wait()

    def chip_at(dx, dy):
        return lax.rem(chip_x + dx, 4) * 4 + lax.rem(chip_y + dy, 4)

    def gather_start(phase, view):
        mine = view(chip, core)
        for j in reversed(range(15)):
            pltpu.make_async_remote_copy(
                src_ref=mine,
                dst_ref=mine,
                send_sem=ph_send.at[phase],
                recv_sem=near_recv.at[phase, j],
                device_id=(z, chip_at(*OFFSETS[j]) * 2 + core),
                device_id_type=MESH,
            ).start()
        to_pair(phase, mine)

    def to_pair(phase, ref):
        pltpu.make_async_remote_copy(
            src_ref=ref,
            dst_ref=ref,
            send_sem=ph_send.at[phase],
            recv_sem=pair_recv.at[phase],
            device_id=(z, chip * 2 + 1 - core),
            device_id_type=MESH,
        ).start()

    def gather_finish(phase, view, sixteen):
        for j in range(15):
            dx, dy = OFFSETS[j]
            ref = view(chip_at(4 - dx, 4 - dy), core)
            wait_bytes(ref, near_recv.at[phase, j])
            to_pair(phase, ref)
        wait_bytes(sixteen, pair_recv.at[phase])

    def gather_left(phase, sixteen, fifteen):
        wait_bytes(sixteen, ph_send.at[phase])
        wait_bytes(fifteen, ph_send.at[phase])

    def scatter_start(phase, src, dst):
        def one(peer):
            pltpu.make_async_remote_copy(
                src_ref=src.at[peer // 4, lax.rem(peer, 4)],
                dst_ref=dst.at[s],
                send_sem=ph_send.at[phase],
                recv_sem=ph_recv.at[phase],
                device_id=(z, peer),
                device_id_type=MESH,
            ).start()

        for j in reversed(range(15)):
            base = chip_at(*OFFSETS[j]) * 2
            one(base + core)
            one(base + 1 - core)
        one(chip * 2 + 1 - core)

    def scatter_wait(sem, phase, dst):
        wait_bytes(dst.at[pl.ds(0, NS - 1)], sem.at[phase])

    part = lax.dot_general(
        normed[...], wall[...].reshape(128, D), RHS_T, preferred_element_type=F32
    )
    pj_view = lambda where, which: pj.at[which, where]
    pj[core, chip] = part.astype(BF16)
    gather_start(0, pj_view)
    send_own(o_hop)
    for c in range(8):
        rows = iota((128, CB), 0)
        lanes = rows % 16
        target = 80 * c + 10 * ((rows // 16 + z) % NZ) + lanes
        hit = (target == iota((128, CB), 1)) & (lanes < 10)
        selo[pl.ds(128 * c, 128), :] = jnp.where(hit, 1.0, 0.0).astype(BF16)
    col_block = lax.rem(s, 4)
    lane = iota((128, CB), 0)
    head_of = (col_block * 5 + iota((128, CB), 1) // 128) // 2
    emat[...] = jnp.where((lane % 16 == head_of) & (lane < 48), 1.0, 0.0).astype(BF16)
    kn[...] = jnp.zeros_like(kn)
    vn[...] = jnp.zeros_like(vn)
    loads[0].wait()
    gather_finish(0, pj_view, pj.at[0])

    groups = jnp.concatenate(
        [
            pj[c % 2].reshape(8, 2, ROWS, 128)[:, c // 2].reshape(8 * ROWS, 128)
            for c in range(4)
        ],
        axis=1,
    )
    proj = jnp.dot(groups, selq[...], preferred_element_type=F32)

    def unit(u):
        g, c = u // 3, u % 3
        return proj[ROWS * g : ROWS * (g + 1), 128 * c : 128 * (c + 1)]

    def turned(v):
        return v * cosb[...] + pltpu.roll(v, 64, 1) * sinb[...]

    for h in range(H):
        qs[pl.ds(ROWS * h, ROWS), pl.ds(0, 128)] = (
            turned(unit(2 * h)).astype(BF16) * jnp.asarray(HD ** -0.5, BF16)
        )
        qs[pl.ds(ROWS * h, ROWS), pl.ds(128, 128)] = (
            unit(2 * h + 1).astype(BF16) * jnp.asarray(HD ** -0.5, BF16)
        )
    kn[pl.ds(0, ROWS), pl.ds(0, 128)] = turned(unit(20)).astype(BF16)
    kn[pl.ds(0, ROWS), pl.ds(128, 128)] = unit(21).astype(BF16)
    vn[pl.ds(0, ROWS), pl.ds(0, 128)] = unit(22).astype(BF16)
    vn[pl.ds(0, ROWS), pl.ds(128, 128)] = unit(23).astype(BF16)
    fresh[:, pl.ds(0, HD)] = kn[pl.ds(0, ROWS), :]
    fresh[:, pl.ds(HD, HD)] = vn[pl.ds(0, ROWS), :]

    send_on(o_hop)

    score_n = lax.dot_general(qs[...], kn[...], RHS_T, preferred_element_type=F32)
    score_n = (score_n.reshape(H, ROWS, 128) + biasn[...][None]).reshape(H * ROWS, 128)
    scn[...] = score_n
    mx[...] = score_n

    def score_block(kb, carry):
        keys = kv[pl.ds(kb * 2, 2), :, pl.ds(0, HD)].reshape(256, HD)
        value = lax.dot_general(qs[...], keys, RHS_T, preferred_element_type=F32)
        value = (value.reshape(H, ROWS, 256) + bias[kb][None]).reshape(H * ROWS, 256)
        sc[kb] = value
        mx[...] = jnp.maximum(mx[...], jnp.maximum(value[:, :128], value[:, 128:]))
        return carry

    lax.fori_loop(0, 8, score_block, 0)
    peak = jnp.max(mx[...], axis=1, keepdims=True)
    mx[...] = jnp.broadcast_to(peak, mx.shape)
    weight = jnp.exp(scn[...] - mx[...])
    lx[...] = weight
    acc[...] = jnp.dot(weight.astype(BF16), vn[...], preferred_element_type=F32)

    def value_block(kb, carry):
        left = jnp.exp(sc[kb, :, pl.ds(0, 128)] - mx[...])
        right = jnp.exp(sc[kb, :, pl.ds(128, 128)] - mx[...])
        lx[...] += left + right
        both = jnp.concatenate([left.astype(BF16), right.astype(BF16)], axis=1)
        values = kv[pl.ds(kb * 2, 2), :, pl.ds(HD, HD)].reshape(256, HD)
        acc[...] += jnp.dot(both, values, preferred_element_type=F32)
        return carry

    lax.fori_loop(0, 8, value_block, 0)
    total = jnp.sum(lx[...], axis=1, keepdims=True)
    level = mx[...] + jnp.log(jnp.broadcast_to(total, mx.shape))
    mixed = acc[...] / total
    lane_h = iota((ROWS, 128), 1)
    table = jnp.zeros((ROWS, 128), F32)
    for h in range(H):
        table = jnp.where(lane_h % 16 == h, level[ROWS * h : ROWS * (h + 1)], table)
        for side in range(2):
            u = 2 * h + side
            piece = mixed[ROWS * h : ROWS * (h + 1), 128 * side : 128 * (side + 1)]
            rs_s[:, u // 5, :, pl.ds(128 * (u % 5), 128)] = piece.reshape(8, 8, 128).astype(BF16)
    first = table.astype(BF16).astype(F32)
    second = (table - first).astype(BF16).astype(F32)
    third = table - first - second
    table = jnp.where(lane_h < 16, first, jnp.where(lane_h < 32, second, third))
    table = jnp.where(lane_h % 16 < H, table, 0.0).reshape(8, 8, 128).astype(BF16)
    for c in range(4):
        rs_s[:, c, :, pl.ds(CB, 128)] = table

    scatter_start(1, rs_s, rs_r)
    rs_r[s] = rs_s[s // 4, lax.rem(s, 4)]

    def write_block(kb, carry):
        news = lax.dot_general(place[kb], fresh[...], (((0,), (0,)), ((), ())), preferred_element_type=F32)
        ones = jnp.ones((ROWS, 2 * HD), BF16)
        hits = lax.dot_general(place[kb], ones, (((0,), (0,)), ((), ())), preferred_element_type=F32)
        olds = kv[pl.ds(kb * 2, 2)].reshape(2 * PAGE, 2 * HD).astype(F32)
        value = jnp.where(hits > 0.5, news, olds).astype(BF16)
        pool_ref[pl.ds(kb * 2, 2)] = value.reshape(2, PAGE, 2 * HD)
        return carry

    lax.fori_loop(0, 8, write_block, 0)
    wall[...] = jnp.zeros_like(wall)
    wall[0, pl.ds(0, 10), :] = ow_ref[...]
    for away in (1, 3, 4):
        arrived(o_hop, away)
    for d in range(1, NZ):
        wall[d, pl.ds(0, 10), :] = wo[d]
    scatter_wait(ph_recv, 1, rs_r)
    levels = rs_r[:, :, pl.ds(CB, 128)].astype(F32).reshape(NS * 8, 128).astype(BF16)
    levels = jnp.dot(levels, emat[...], preferred_element_type=F32).reshape(NS, 8, CB)
    factor = jnp.exp(levels - jnp.max(levels, axis=0, keepdims=True))
    number = jnp.sum(factor * rs_r[:, :, pl.ds(0, CB)].astype(F32), axis=0)
    attended = number / jnp.sum(factor, axis=0)

    att_view = lambda where, which: att.at[which, where]
    att[core, chip] = attended.astype(BF16)
    gather_start(2, att_view)
    gather_finish(2, att_view, att.at[0])
    part = jnp.zeros((ROWS, 128), F32)
    for c in range(4):
        left_rows = att[c % 2].astype(F32).reshape(8, 2, 8, CB)[:, c // 2].reshape(ROWS, CB)
        part += lax.dot_general(
            left_rows.astype(BF16), wall[:, :, pl.ds(CB * c, CB)].reshape(128, CB), RHS_T,
            preferred_element_type=F32,
        )

    ho_view = lambda where, which: ho.at[which, where]
    ho[core, chip] = part.astype(BF16)
    gather_start(3, ho_view)
    loads[1].wait()
    loads[2].wait()
    gain = gains(mg_ref)
    gather_finish(3, ho_view, ho.at[0])
    groups = jnp.concatenate(
        [
            ho[c % 2].reshape(4, 4, ROWS, 128)[:, c // 2].reshape(4 * ROWS, 128)
            for c in range(8)
        ],
        axis=1,
    )
    heads_out = jnp.dot(groups, selo[...], preferred_element_type=F32)
    square = jnp.zeros((ROWS, 1), F32)
    pieces = []
    for c in range(4):
        x = tokr[:, pl.ds(CB * c, CB)]
        x = (x + heads_out[ROWS * c : ROWS * (c + 1)]).astype(BF16).astype(F32)
        pieces.append(x)
        resid[:, c] = x.reshape(8, 8, CB)
        square += jnp.sum(x * x, axis=1, keepdims=True)
    scale = lax.rsqrt(square * (1.0 / D) + 1e-06)
    gate = jnp.zeros((ROWS, FFL), F32)
    lift = jnp.zeros((ROWS, FFL), F32)
    for c in range(4):
        cols = pl.ds(CB * c, CB)
        entry = (pieces[c] * scale * gain[:, CB * c : CB * (c + 1)]).astype(BF16)
        gate += lax.dot_general(entry, gu[0, :, cols], RHS_T, preferred_element_type=F32)
        lift += lax.dot_general(entry, gu[1, :, cols], RHS_T, preferred_element_type=F32)
    inner = np.float32(np.sqrt(2.0 / np.pi)) * (gate + 0.044715 * (gate * gate * gate))
    hidden = (0.5 * gate * (1.0 + jnp.tanh(inner)) * lift).astype(BF16)
    for c in range(4):
        value = jnp.dot(hidden, dn[:, pl.ds(CB * c, CB)], preferred_element_type=F32)
        r2_s[:, c] = value.reshape(8, 8, CB).astype(BF16)

    scatter_start(4, r2_s, r2_r)
    r2_r[s] = r2_s[s // 4, lax.rem(s, 4)]
    scatter_wait(ph_recv, 4, r2_r)
    done = jnp.sum(r2_r[...].astype(F32), axis=0) + resid[s // 4, lax.rem(s, 4)]

    def out_view(where, which):
        index = where * 2 + which
        cols = pl.ds(pl.multiple_of(lax.rem(index, 4) * CB, 128), CB)
        return out_ref.at[index // 4, :, cols]

    out_ref[s // 4, :, pl.ds(pl.multiple_of(lax.rem(s, 4) * CB, 128), CB)] = done.astype(BF16)
    gather_start(5, out_view)
    left(q_hop)
    left(o_hop)
    gather_left(0, pj.at[0], pj.at[0, pl.ds(0, 15)])
    gather_left(2, att.at[0], att.at[0, pl.ds(0, 15)])
    gather_left(3, ho.at[0], ho.at[0, pl.ds(0, 15)])
    scatter_wait(ph_send, 1, rs_r)
    scatter_wait(ph_send, 4, r2_r)
    gather_finish(5, out_view, att.at[0])
    gather_left(5, att.at[0], att.at[0, pl.ds(0, 15)])


def body(
    tokens,
    attn_gain,
    qkv_weight,
    out_weight,
    mlp_gain,
    gate_up,
    down_weight,
    kv_pool,
    cache_len,
    page_table,
):
    freq = np.arange(64, dtype=np.float64)
    inverse = (10000.0 ** (-freq / 64)).astype(np.float32)
    inverse = jnp.asarray(np.concatenate([inverse, inverse])[None, :])
    vmem = pl.BlockSpec(memory_space=pltpu.VMEM)
    smem = pl.BlockSpec(memory_space=pltpu.SMEM)
    hbm = pl.BlockSpec(memory_space=pltpu.HBM)
    dma = pltpu.SemaphoreType.DMA
    blocks, written_pool = pl.pallas_call(
        layer_kernel,
        out_shape=(
            jax.ShapeDtypeStruct((8, 8, D), BF16),
            jax.ShapeDtypeStruct((SLOTS, PAGE, 2 * HD), BF16),
        ),
        in_specs=[vmem] * 5 + [hbm] * 3 + [smem, vmem, vmem],
        out_specs=(vmem, vmem),
        scratch_shapes=[
            pltpu.VMEM((R, NEW, D), F32),
            pltpu.VMEM((ROWS, D), F32),
            pltpu.VMEM((ROWS, D), BF16),
            pltpu.VMEM((NZ, 12, D), BF16),
            pltpu.VMEM((NZ, 16, D), BF16),
            pltpu.VMEM((NZ, 10, D), BF16),
            pltpu.VMEM((2, 16, ROWS, 128), BF16),
            pltpu.VMEM((512, 384), BF16),
            pltpu.VMEM((1024, CB), BF16),
            pltpu.VMEM((ROWS, 128), F32),
            pltpu.VMEM((ROWS, 128), F32),
            pltpu.VMEM((8, ROWS, 256), F32),
            pltpu.VMEM((ROWS, 128), F32),
            pltpu.VMEM((8, ROWS, 256), BF16),
            pltpu.VMEM((SLOTS, PAGE, 2 * HD), BF16),
            pltpu.VMEM((2, FFL, D), BF16),
            pltpu.VMEM((FFL, D), BF16),
            pltpu.VMEM((H * ROWS, HD), BF16),
            pltpu.VMEM((128, HD), BF16),
            pltpu.VMEM((128, HD), BF16),
            pltpu.VMEM((ROWS, 2 * HD), BF16),
            pltpu.VMEM((8, H * ROWS, 256), F32),
            pltpu.VMEM((H * ROWS, 128), F32),
            pltpu.VMEM((H * ROWS, 128), F32),
            pltpu.VMEM((H * ROWS, 128), F32),
            pltpu.VMEM((H * ROWS, HD), F32),
            pltpu.VMEM((8, 4, 8, CB + 128), BF16),
            pltpu.VMEM((NS, 8, CB + 128), BF16),
            pltpu.VMEM((128, CB), BF16),
            pltpu.VMEM((2, 16, 8, CB), BF16),
            pltpu.VMEM((2, 16, ROWS, 128), BF16),
            pltpu.VMEM((8, 4, 8, CB), F32),
            pltpu.VMEM((8, 4, 8, CB), BF16),
            pltpu.VMEM((NS, 8, CB), BF16),
            dma((3,)),
            dma((2, 4, 2)),
            dma((2, 4, 2)),
            dma((2, 4, 2)),
            dma((2, 4, 2)),
            dma((6,)),
            dma((6,)),
            dma((6, 15)),
            dma((6,)),
        ],
        compiler_params=pltpu.CompilerParams(
            collective_id=0, has_side_effects=True, vmem_limit_bytes=60 * 1024 * 1024
        ),
        name="layer",
    )(
        tokens,
        attn_gain.reshape(D // 128, 128),
        qkv_weight,
        out_weight,
        mlp_gain.reshape(D // 128, 128),
        gate_up,
        down_weight,
        kv_pool,
        cache_len,
        page_table,
        inverse,
    )
    return (blocks.reshape(R, NEW, D), written_pool)


def solution(mesh):
    in_specs = (
        P("dp", None, None),
        P(),
        P(("seq", "dp"), None),
        P(("seq", "dp"), None),
        P(),
        P(None, "seq", None),
        P("seq", None),
        P(("dp", "seq"), None, None),
        P("dp"),
        P("dp", None),
    )
    out_specs = (P("dp", None, None), P(("dp", "seq"), None, None))
    return jax.shard_map(body, mesh=mesh, in_specs=in_specs, out_specs=out_specs, check_vma=False)
```

time: 94.4 us -> 79.4 us (0.84)
  Pallas kernels: 88.8 us -> 73.7 us
    pallas_call x2 -> x1, Pallas kernels: 88.8 us -> 73.7 us  [body(): pl.pallas_call(layer_kernel, out_shape=(jax.ShapeDtypeStruct((8, 8, D), B...]
    unnamed x0 -> x1, local copies, waits for them, and re-layouts: none -> 3.09 us
    reshape x3 -> x1, local copies, waits for them, and re-layouts: 3.47 us -> 1.78 us  [body(): return (blocks.reshape(R, NEW, D), written_pool)]
    transpose x1 -> x0, local copies, waits for them, and re-layouts: 1.1 us -> none  [body(): blocks.reshape(4, 2, 4, 8, CB).transpose(1, 3, 0, 2, 4).reshape(R, NEW, D)]
where the time goes in v2:
time: 79.4 us; the launch traced here: 79.2 us
  Pallas kernels  73.7 us (93%)
  local copies, waits for them, and re-layouts  4.87 us (6%)
    pallas_call x1, Pallas kernels, body(): pl.pallas_call(layer_kernel, out_shape=(jax.ShapeDtypeStruct((8, 8, D), B...  73.7 us
    unnamed x1, local copies, waits for them, and re-layouts  3.09 us
    reshape x1, local copies, waits for them, and re-layouts, body(): return (blocks.reshape(R, NEW, D), written_pool)  1.78 us

profile of v2, /device:TPU:1, one launch (start us, length us, event | category | flops | bytes accessed | tf_op | source)
XLA Modules:
  0.0 79.2 jit_solution(11794021831593288674)
XLA Ops:
  0.6 73.7 %layer.1 = (bf16[8,8,2560]{2,1,0:T(8,128)(2,1)}, bf16[16,128,512]{2,1,0:T(8,128)(2,1)}) custom-call(bf16[16,4,2560]{2,1,0:T(4,128)(2,1)} %tok_ref.1, f32[20,128]{1,0:T(8,128)} %bitcast.2, bf16[12,2560]{1,0:T(8,128)(2,1)} %qkv_ref.1, bf16[10,2560]{1,0:T(8,128)(2,1)} %ow_ref.1, f32[20,128]{1,0:T(8,128)} %bitcast.3, bf16[2,240,2560]{2,1,0:T(8,128)(2,1)} %gu_hbm.1, ...), custom_call_target="tpu_custom_call" | custom-call | tf_op jit(solution)/shard_map/layer/pallas_call | solution.py:483
  74.4 1.8 %reshape.15 = bf16[16,4,2560]{2,1,0:T(4,128)(2,1)} reshape(bf16[8,8,2560]{2,1,0:T(8,128)(2,1)} %get-tuple-element.4) | data formatting | bytes 655360 | tf_op jit(solution)/shard_map/reshape | solution.py:553
  76.1 3.1 %copy.14 = bf16[16,128,512]{2,1,0:T(8,128)(2,1)} copy(bf16[16,128,512]{2,1,0:T(8,128)(2,1)} %get-tuple-element.9) | data formatting | bytes 4194304
